TPU v7x, 32 devices: a whole 2x2x4 slice. The times are simulated.
32 devices in a mesh: shard: 4 (over z), context: 2 (over y), tensor: 4 (over x, core).
Axes of the slice: x: 2, y: 2, z: 4, core: 2. Of those that a mesh axis runs over, the one named last changes fastest.
Arguments:
- tokens: bfloat16 [16, 1024, 1024], P('shard', 'context'), may hold values from -6 to 6
- cotangent: bfloat16 [16, 1024, 1024], P('shard', 'context'), may hold values from -6 to 6
- adapter_index: int32 [16], P('shard'), may hold values from 0 to 7, as said below
- ln1_gain: float32 [1024], replicated, may hold values from 0.5 to 1.5
- ln1_bias: float32 [1024], replicated, may hold values from -1.5 to 1.5
- ln2_gain: float32 [1024], replicated, may hold values from 0.5 to 1.5
- ln2_bias: float32 [1024], replicated, may hold values from -1.5 to 1.5
- layer_scale: float32 [2, 1024], replicated, may hold values from 0.4 to 1.2
- w_qkv: bfloat16 [1024, 3, 1024], P(('shard', 'context'), None, 'tensor'), may hold values from -0.1875 to 0.1875
- w_proj: bfloat16 [1024, 1024], P(('shard', 'context'), 'tensor'), may hold values from -0.5 to 0.5
- w_fc1: bfloat16 [1024, 4096], P(('shard', 'context'), 'tensor'), may hold values from -0.1875 to 0.1875
- w_fc2: bfloat16 [1024, 4096], P(('shard', 'context'), 'tensor'), may hold values from -0.09375 to 0.09375
- down_in: bfloat16 [8, 4, 1024, 16], replicated, may hold values from -0.1875 to 0.1875
- qkv_up: bfloat16 [8, 3, 16, 1024], P(None, None, None, 'tensor'), may hold values from -1.5 to 1.5
- fc1_up: bfloat16 [8, 16, 4096], P(None, None, 'tensor'), may hold values from -1.5 to 1.5
- proj_down: bfloat16 [8, 1024, 16], P(None, 'tensor'), may hold values from -0.5 to 0.5
- fc2_down: bfloat16 [8, 4096, 16], P(None, 'tensor'), may hold values from -0.09375 to 0.09375
- out_up: bfloat16 [8, 2, 16, 1024], replicated, may hold values from -1.5 to 1.5
Outputs:
- result: bfloat16 [16, 1024, 1024], P('shard', 'context')
- input_grad: float32 [16, 1024, 1024], P('shard', 'context')
- down_in_grad: float32 [8, 4, 1024, 16], replicated
- qkv_up_grad: float32 [8, 3, 16, 1024], P(None, None, None, 'tensor')
- fc1_up_grad: float32 [8, 16, 4096], P(None, None, 'tensor')
- proj_down_grad: float32 [8, 1024, 16], P(None, 'tensor')
- fc2_down_grad: float32 [8, 4096, 16], P(None, 'tensor')
- out_up_grad: float32 [8, 2, 16, 1024], replicated
Inputs may be any that keep to these rules, and one draw needn't show every extreme that they name: `adapter_index`: every adapter index is used by exactly 2 images.
All inputs are finite; a program needn't handle non-finite values.
Results may differ from a plain program's by a relative error of at most 0.015.
The roundings to bfloat16 on the way count: a program that leaves them out, or rounds other values in their place, can miss the bound.
Values may be sent and summed in bfloat16 or wider, within the bound.
No kernel may reach another device: no remote copies, remote signals or barrier semaphores. Data moves between devices by JAX's collectives and lax.ppermute only.
A program may use at most 256 MiB of HBM per device.

v0:
```python
import math
import jax
import jax.numpy as jnp
from jax import lax
from jax.sharding import PartitionSpec as P

HEAD_DIM = 64
eps_norm = 1e-06


def normalize(values, norm_gain, norm_shift):
    centre = values - jnp.mean(values, axis=-1, keepdims=True)
    inverse = lax.rsqrt(jnp.mean(centre * centre, axis=-1, keepdims=True) + eps_norm)
    unit_values = centre * inverse
    return (unit_values * norm_gain + norm_shift, unit_values, inverse)


def norm_back(grad_out, unit_values, inverse, norm_gain):
    scaled = grad_out * norm_gain
    centred = scaled - jnp.mean(scaled, axis=-1, keepdims=True)
    return inverse * (
        centred - unit_values * jnp.mean(scaled * unit_values, axis=-1, keepdims=True)
    )


def per_device(
    tokens,
    cotangent,
    adapter_index,
    ln1_gain,
    ln1_bias,
    ln2_gain,
    ln2_bias,
    layer_scale,
    w_qkv,
    w_proj,
    w_fc1,
    w_fc2,
    down_in,
    qkv_up,
    fc1_up,
    proj_down,
    fc2_down,
    out_up,
):
    images, row_count, model_width = tokens.shape
    adapter_count = down_in.shape[0]
    choose = (adapter_index[:, None] == jnp.arange(adapter_count, dtype=jnp.int32)[None, :]).astype(
        jnp.bfloat16
    )
    choose_float = choose.astype(jnp.float32)

    def select_rows(stacked):
        return jnp.einsum(
            "ia,a...->i...", choose, stacked, preferred_element_type=jnp.float32
        ).astype(jnp.bfloat16)

    def collect(per_image):
        return jnp.einsum("ia,i...->a...", choose_float, per_image, precision=lax.Precision.HIGHEST)

    sel_down = select_rows(down_in)
    sel_qkv = select_rows(qkv_up)
    sel_fc1 = select_rows(fc1_up)
    sel_proj = select_rows(proj_down)
    sel_fc2 = select_rows(fc2_down)
    sel_out = select_rows(out_up)
    score_scale = 1.0 / math.sqrt(HEAD_DIM)
    attn_full, proj_full = (
        lax.all_gather(w_qkv, ("shard", "context"), axis=0, tiled=True),
        lax.all_gather(w_proj, ("shard", "context"), axis=0, tiled=True),
    )
    fc1_full, fc2_full = (
        lax.all_gather(w_fc1, ("shard", "context"), axis=0, tiled=True),
        lax.all_gather(w_fc2, ("shard", "context"), axis=0, tiled=True),
    )
    resid = tokens.astype(jnp.float32)
    normed, unit_one, inverse_one = normalize(resid, ln1_gain, ln1_bias)
    normed_low = normed.astype(jnp.bfloat16)
    rank_qkv = jnp.einsum(
        "ild,ikdr->iklr", normed_low, sel_down[:, :3], preferred_element_type=jnp.float32
    ).astype(jnp.bfloat16)
    projected = jnp.einsum(
        "ild,dkc->iklc", normed_low, attn_full, preferred_element_type=jnp.float32
    )
    projected = projected + jnp.einsum(
        "iklr,ikrc->iklc", rank_qkv, sel_qkv, preferred_element_type=jnp.float32
    )
    projected_low = projected.astype(jnp.bfloat16)
    local_width = projected_low.shape[-1]
    head_count = local_width // HEAD_DIM
    queries = projected_low[:, 0].reshape(images, row_count, head_count, HEAD_DIM)
    keys_all, values_all = (
        lax.all_gather(projected_low[:, 1], "context", axis=1, tiled=True),
        lax.all_gather(projected_low[:, 2], "context", axis=1, tiled=True),
    )
    key_heads = keys_all.reshape(images, -1, head_count, HEAD_DIM)
    value_heads = values_all.reshape(images, -1, head_count, HEAD_DIM)
    scores = (
        jnp.einsum("iqhe,ikhe->ihqk", queries, key_heads, preferred_element_type=jnp.float32)
        * score_scale
    )
    row_peak = jnp.max(scores, axis=-1, keepdims=True)
    exp_scores = jnp.exp(scores - row_peak)
    exp_total = jnp.sum(exp_scores, axis=-1, keepdims=True)
    log_total = row_peak + jnp.log(exp_total)
    probabilities = (exp_scores / exp_total).astype(jnp.bfloat16)
    mixed_heads = jnp.einsum(
        "ihqk,ikhe->iqhe", probabilities, value_heads, preferred_element_type=jnp.float32
    )
    mixed_low = mixed_heads.reshape(images, row_count, local_width).astype(jnp.bfloat16)
    proj_part = jnp.einsum("ilc,dc->ild", mixed_low, proj_full, preferred_element_type=jnp.float32)
    proj_rank_part = jnp.einsum(
        "ilc,icr->ilr", mixed_low, sel_proj, preferred_element_type=jnp.float32
    )
    proj_total, proj_rank_total = lax.psum((proj_part, proj_rank_part), "tensor")
    proj_rank = proj_rank_total.astype(jnp.bfloat16)
    attn_out = proj_total + jnp.einsum(
        "ilr,ird->ild", proj_rank, sel_out[:, 0], preferred_element_type=jnp.float32
    )
    hidden_one = resid + layer_scale[0] * attn_out
    normed_two, unit_two, inverse_two = normalize(hidden_one, ln2_gain, ln2_bias)
    normed_two_low = normed_two.astype(jnp.bfloat16)
    fc1_rank = jnp.einsum(
        "ild,idr->ilr", normed_two_low, sel_down[:, 3], preferred_element_type=jnp.float32
    ).astype(jnp.bfloat16)
    preact = jnp.einsum("ild,df->ilf", normed_two_low, fc1_full, preferred_element_type=jnp.float32)
    preact = preact + jnp.einsum(
        "ilr,irf->ilf", fc1_rank, sel_fc1, preferred_element_type=jnp.float32
    )
    activation = jax.nn.gelu(preact, approximate=False).astype(jnp.bfloat16)
    mlp_part = jnp.einsum("ilf,df->ild", activation, fc2_full, preferred_element_type=jnp.float32)
    fc2_rank_part = jnp.einsum(
        "ilf,ifr->ilr", activation, sel_fc2, preferred_element_type=jnp.float32
    )
    mlp_total, fc2_rank_total = (
        lax.psum(mlp_part.astype(jnp.bfloat16), "tensor").astype(jnp.float32),
        lax.psum(fc2_rank_part.astype(jnp.bfloat16), "tensor").astype(jnp.float32),
    )
    fc2_rank = fc2_rank_total.astype(jnp.bfloat16)
    branch = mlp_total + jnp.einsum(
        "ilr,ird->ild", fc2_rank, sel_out[:, 1], preferred_element_type=jnp.float32
    )
    result = (hidden_one + layer_scale[1] * branch).astype(jnp.bfloat16)
    upstream = cotangent.astype(jnp.float32)
    fc1_back, fc2_back = (
        lax.all_gather(w_fc1, ("shard", "context"), axis=0, tiled=True),
        lax.all_gather(w_fc2, ("shard", "context"), axis=0, tiled=True),
    )
    grad_branch = (upstream * layer_scale[1]).astype(jnp.bfloat16)
    grad_fc2_rank = jnp.einsum(
        "ild,ird->ilr", grad_branch, sel_out[:, 1], preferred_element_type=jnp.float32
    ).astype(jnp.bfloat16)
    out_grad_fc2 = jnp.einsum(
        "ilr,ild->ird", fc2_rank, grad_branch, preferred_element_type=jnp.float32
    )
    grad_activation = jnp.einsum(
        "ild,df->ilf", grad_branch, fc2_back, preferred_element_type=jnp.float32
    )
    grad_activation = grad_activation + jnp.einsum(
        "ilr,ifr->ilf", grad_fc2_rank, sel_fc2, preferred_element_type=jnp.float32
    )
    fc2_down_part = jnp.einsum(
        "ilf,ilr->ifr", activation, grad_fc2_rank, preferred_element_type=jnp.float32
    )
    normal_cdf = 0.5 * (1.0 + lax.erf(preact * (1.0 / math.sqrt(2.0))))
    normal_density = jnp.exp(-0.5 * preact * preact) * (1.0 / math.sqrt(2.0 * math.pi))
    grad_preact = (grad_activation * (normal_cdf + preact * normal_density)).astype(jnp.bfloat16)
    fc1_up_part = jnp.einsum(
        "ilr,ilf->irf", fc1_rank, grad_preact, preferred_element_type=jnp.float32
    )
    normed_two_part = jnp.einsum(
        "ilf,df->ild", grad_preact, fc1_back, preferred_element_type=jnp.float32
    )
    fc1_rank_part = jnp.einsum(
        "ilf,irf->ilr", grad_preact, sel_fc1, preferred_element_type=jnp.float32
    )
    grad_normed_two, grad_fc1_total = lax.psum((normed_two_part, fc1_rank_part), "tensor")
    grad_fc1_rank = grad_fc1_total.astype(jnp.bfloat16)
    grad_normed_two = grad_normed_two + jnp.einsum(
        "ilr,idr->ild", grad_fc1_rank, sel_down[:, 3], preferred_element_type=jnp.float32
    )
    fc1_down_part = jnp.einsum(
        "ild,ilr->idr", normed_two_low, grad_fc1_rank, preferred_element_type=jnp.float32
    )
    grad_hidden = upstream + norm_back(grad_normed_two, unit_two, inverse_two, ln2_gain)
    qkv_back, proj_back = (
        lax.all_gather(w_qkv, ("shard", "context"), axis=0, tiled=True),
        lax.all_gather(w_proj, ("shard", "context"), axis=0, tiled=True),
    )
    grad_attn = (grad_hidden * layer_scale[0]).astype(jnp.bfloat16)
    grad_proj_rank = jnp.einsum(
        "ild,ird->ilr", grad_attn, sel_out[:, 0], preferred_element_type=jnp.float32
    ).astype(jnp.bfloat16)
    out_grad_proj = jnp.einsum(
        "ilr,ild->ird", proj_rank, grad_attn, preferred_element_type=jnp.float32
    )
    grad_mixed = jnp.einsum("ild,dc->ilc", grad_attn, proj_back, preferred_element_type=jnp.float32)
    grad_mixed = grad_mixed + jnp.einsum(
        "ilr,icr->ilc", grad_proj_rank, sel_proj, preferred_element_type=jnp.float32
    )
    grad_mixed_low = grad_mixed.astype(jnp.bfloat16)
    proj_down_part = jnp.einsum(
        "ilc,ilr->icr", mixed_low, grad_proj_rank, preferred_element_type=jnp.float32
    )
    keys_back, values_back = (keys_all, values_all)
    key_heads_back = keys_back.reshape(images, -1, head_count, HEAD_DIM)
    value_heads_back = values_back.reshape(images, -1, head_count, HEAD_DIM)
    grad_heads = grad_mixed_low.reshape(images, row_count, head_count, HEAD_DIM)
    scores_again = (
        jnp.einsum("iqhe,ikhe->ihqk", queries, key_heads_back, preferred_element_type=jnp.float32)
        * score_scale
    )
    probs_again = jnp.exp(scores_again - log_total)
    grad_probs = jnp.einsum(
        "iqhe,ikhe->ihqk", grad_heads, value_heads_back, preferred_element_type=jnp.float32
    )
    row_inner = jnp.sum(probs_again * grad_probs, axis=-1, keepdims=True)
    grad_scores = (probs_again * (grad_probs - row_inner)).astype(jnp.bfloat16)
    grad_queries = (
        jnp.einsum(
            "ihqk,ikhe->iqhe", grad_scores, key_heads_back, preferred_element_type=jnp.float32
        )
        * score_scale
    )
    key_part = (
        jnp.einsum("ihqk,iqhe->ikhe", grad_scores, queries, preferred_element_type=jnp.float32)
        * score_scale
    )
    value_part = jnp.einsum(
        "ihqk,iqhe->ikhe",
        probs_again.astype(jnp.bfloat16),
        grad_heads,
        preferred_element_type=jnp.float32,
    )
    key_grad, value_grad = (
        lax.psum_scatter(
            key_part.reshape(images, -1, local_width), "context", scatter_dimension=1, tiled=True
        ),
        lax.psum_scatter(
            value_part.reshape(images, -1, local_width), "context", scatter_dimension=1, tiled=True
        ),
    )
    grad_projected = jnp.stack(
        [grad_queries.reshape(images, row_count, local_width), key_grad, value_grad], axis=1
    ).astype(jnp.bfloat16)
    qkv_up_part = jnp.einsum(
        "iklr,iklc->ikrc", rank_qkv, grad_projected, preferred_element_type=jnp.float32
    )
    normed_part = jnp.einsum(
        "iklc,dkc->ild", grad_projected, qkv_back, preferred_element_type=jnp.float32
    )
    rank_part = jnp.einsum(
        "iklc,ikrc->iklr", grad_projected, sel_qkv, preferred_element_type=jnp.float32
    )
    grad_normed, grad_rank_total = lax.psum((normed_part, rank_part), "tensor")
    grad_rank = grad_rank_total.astype(jnp.bfloat16)
    grad_normed = grad_normed + jnp.einsum(
        "iklr,ikdr->ild", grad_rank, sel_down[:, :3], preferred_element_type=jnp.float32
    )
    qkv_down_part = jnp.einsum(
        "ild,iklr->ikdr", normed_low, grad_rank, preferred_element_type=jnp.float32
    )
    input_grad = grad_hidden + norm_back(grad_normed, unit_one, inverse_one, ln1_gain)
    down_total = collect(jnp.concatenate([qkv_down_part, fc1_down_part[:, None]], axis=1))
    qkv_up_total = collect(qkv_up_part)
    fc1_up_total = collect(fc1_up_part)
    proj_down_total = collect(proj_down_part)
    fc2_down_total = collect(fc2_down_part)
    out_up_total = collect(jnp.stack([out_grad_proj, out_grad_fc2], axis=1))
    adapter_sums = lax.psum(
        (down_total, qkv_up_total, fc1_up_total, proj_down_total, fc2_down_total, out_up_total),
        ("shard", "context"),
    )
    return (
        result,
        input_grad,
        adapter_sums[0],
        adapter_sums[1],
        adapter_sums[2],
        adapter_sums[3],
        adapter_sums[4],
        adapter_sums[5],
    )


def solution(mesh):
    placed = (
        P("shard", "context", None),
        P("shard", "context", None),
        P("shard"),
        P(),
        P(),
        P(),
        P(),
        P(),
        P(("shard", "context"), None, "tensor"),
        P(("shard", "context"), "tensor"),
        P(("shard", "context"), "tensor"),
        P(("shard", "context"), "tensor"),
        P(),
        P(None, None, None, "tensor"),
        P(None, None, "tensor"),
        P(None, "tensor", None),
        P(None, "tensor", None),
        P(),
    )
    return jax.shard_map(
        per_device,
        mesh=mesh,
        in_specs=placed,
        out_specs=(
            P("shard", "context", None),
            P("shard", "context", None),
            P(),
            P(None, None, None, "tensor"),
            P(None, None, "tensor"),
            P(None, "tensor", None),
            P(None, "tensor", None),
            P(),
        ),
        check_vma=False,
    )
```

profile of v0, /device:TPU:0, one launch (start us, length us, event | category | flops | bytes accessed | tf_op | source)
XLA Modules:
  0.0 1194.9 jit_solution(3190369262834206231)
XLA Ops:
  7.3 1.8 copy.26
  10.9 3.0 convert_reduce_fusion
  15.7 2.1 convolution_convert_fusion.3
  17.8 40.0 %all-gather.8.cloned.1.call-done = bf16[1024,3,256]{0,2,1:T(8,128)(2,1)} async-done(((bf16[128,3,256]{0,2,1:T(8,128)(2,1)}), bf16[1024,3,256]{0,2,1:T(8,128)(2,1)}) %all-gather.8.cloned.1.call-update) | async-done | bytes 1572880 | tf_op jit(solution)/shard_map/all_gather | solution.py:69
  57.8 6.1 fusion.53
  65.0 1.7 fusion.135
  68.1 32.2 %all_gather.25 = bf16[1024,256]{1,0:T(8,128)(2,1)S(1)} all-gather(bf16[128,256]{1,0:T(8,128)(2,1)S(1)} %copy-done.55), channel_id=1, replica_groups=mesh['shard'=4,'context'=2,'tensor'=4] {'shard','context'}, dimensions={0}, use_global_device_ids=true | all-gather | bytes 589824 | tf_op jit(solution)/shard_map/all_gather | solution.py:70
  100.3 6.1 all-gather.16.cloned.1.call-done
  106.4 15.7 %multiply_reduce_fusion.1 = (f32[4,4,512]{2,1,0:T(4,128)S(1)}, f32[4,4,512,1024]{3,2,1,0:T(8,128)}) fusion(bf16[4,512,4,64]{1,3,2,0:T(8,128)(2,1)S(1)} %bitcast.147, bf16[4,1024,4,64]{1,3,2,0:T(8,128)(2,1)} %bitcast.149), kind=kOutput, calls=%fused_computation.6 | convolution fusion | flops 1090510848 | bytes 36732928 | tf_op jit(solution)/shard_map/iqhe,ikhe->ihqk/dot_general | solution.py:99
  122.2 14.2 %fusion = f32[4,4,512]{2,1,0:T(4,128)S(1)} fusion(f32[4,4,512,1024]{3,2,1,0:T(8,128)} %get-tuple-element.38, f32[4,4,512]{2,1,0:T(4,128)S(1)} %get-tuple-element.37), kind=kLoop, calls=%fused_computation.5 | loop fusion | flops 25157632 | bytes 33619968 | tf_op jit(solution)/shard_map/reduce_sum | solution.py:104
  136.4 4.7 all-gather.14.cloned.1.call-done
  141.1 14.4 %fusion.55 = bf16[4,4,64,512]{3,2,1,0:T(8,128)(2,1)S(1)} fusion(bf16[4,1024,4,64]{1,3,2,0:T(8,128)(2,1)} %bitcast.153, f32[4,4,512,1024]{3,2,1,0:T(8,128)} %get-tuple-element.38, f32[4,4,512]{2,1,0:T(4,128)S(1)} %fusion, f32[4,4,512]{2,1,0:T(4,128)S(1)} %get-tuple-element.37), kind=kOutput, calls=%fused_computation.92 | convolution fusion | flops 1107820544 | bytes 36765696 | tf_op jit(solution)/shard_map/ihqk,ikhe->iqhe/dot_general | solution.py:107
  155.6 4.7 fusion.69
  163.9 3.4 fusion.59
  167.3 24.9 %all-gather.12.cloned.1.call-done = bf16[1024,1024]{1,0:T(8,128)(2,1)} async-done(((bf16[128,1024]{1,0:T(8,128)(2,1)}), bf16[1024,1024]{1,0:T(8,128)(2,1)}) %all-gather.12.cloned.1.call-update) | async-done | bytes 2097168 | tf_op jit(solution)/shard_map/all_gather | solution.py:74
  192.2 10.7 fusion.42
  203.1 15.5 %all-reduce.20 = bf16[4,512,16]{1,2,0:T(8,128)(2,1)S(1)} all-reduce(f32[4,512,16]{1,2,0:T(8,128)S(1)} %fusion.110), channel_id=1, replica_groups=mesh['shard'=4,'context'=2,'tensor'=4] {'tensor'}, use_global_device_ids=true, to_apply=%region_5.0 | all-reduce | flops 32768 | bytes 196608 | tf_op jit(solution)/shard_map/psum | solution.py:115
  218.6 130.0 %all-reduce.11.cloned.1.call-done = f32[4,512,1024]{2,1,0:T(8,128)} async-done(((f32[4,512,1024]{2,1,0:T(8,128)}), f32[4,512,1024]{2,1,0:T(8,128)}) %all-reduce.11.cloned.1.call-update) | async-done | bytes 8388624 | tf_op jit(solution)/shard_map/psum | solution.py:115
  348.6 6.4 fusion.137
  358.4 2.0 copy-done.6
  361.6 38.2 %all-gather.10.cloned.1.call-done = bf16[1024,1024]{1,0:T(8,128)(2,1)} async-done(((bf16[128,1024]{1,0:T(8,128)(2,1)}), bf16[1024,1024]{1,0:T(8,128)(2,1)}) %all-gather.10.cloned.1.call-update) | async-done | bytes 2097168 | tf_op jit(solution)/shard_map/all_gather | solution.py:73
  399.9 6.9 fusion.48
  406.8 5.5 fusion.51
  412.3 9.0 fusion.28
  421.4 2.0 copy-done.11
  423.4 6.9 fusion.46
  430.7 3.4 fusion.89
  434.1 15.3 %all-reduce.21 = bf16[4,512,16]{1,2,0:T(8,128)(2,1)S(1)} all-reduce(f32[4,512,16]{1,2,0:T(8,128)S(1)} %fusion.89), channel_id=1, replica_groups=mesh['shard'=4,'context'=2,'tensor'=4] {'tensor'}, use_global_device_ids=true, to_apply=%region_11.0 | all-reduce | flops 32768 | bytes 196608 | tf_op jit(solution)/shard_map/psum | solution.py:177
  449.4 134.7 %all-reduce.13.cloned.1.call-done = f32[4,512,1024]{2,1,0:T(8,128)} async-done(((f32[4,512,1024]{2,1,0:T(8,128)}), f32[4,512,1024]{2,1,0:T(8,128)}) %all-reduce.13.cloned.1.call-update) | async-done | bytes 8388624 | tf_op jit(solution)/shard_map/psum | solution.py:177
  584.1 7.4 fusion.134
  591.6 8.1 multiply_convert_fusion.1
  603.5 15.4 %fusion.2 = f32[4,4,64,1024]{3,2,1,0:T(8,128)} fusion(bf16[4,512,4,64]{1,3,2,0:T(8,128)(2,1)S(1)} %bitcast.145, f32[4,4,512,1024]{3,2,1,0:T(8,128)} %get-tuple-element.38, f32[4,4,512]{2,1,0:T(4,128)S(1)} %bitcast.155), kind=kOutput, calls=%fused_computation.8 | convolution fusion | flops 1098907648 | bytes 38830080 | tf_op jit(solution)/shard_map/ihqk,iqhe->ikhe/dot_general | solution.py:229
  618.9 5.5 copy.51
  624.8 22.9 %multiply_reduce_fusion = (f32[4,4,512]{2,1,0:T(4,128)S(1)}, f32[4,4,512,1024]{3,2,1,0:T(8,128)}) fusion(f32[4,4,512,1024]{3,2,1,0:T(8,128)} %get-tuple-element.38, f32[4,4,512]{2,1,0:T(4,128)S(1)} %bitcast.156, bf16[4,512,4,64]{1,3,2,0:T(8,128)(2,1)S(1)} %bitcast.146, bf16[4,1024,4,64]{1,3,2,0:T(8,128)(2,1)S(1)} %bitcast.154), kind=kOutput, calls=%fused_computation.1 | convolution fusion | flops 1107288064 | bytes 70320128 | tf_op jit(solution)/shard_map/iqhe,ikhe->ihqk/dot_general | solution.py:214
  647.7 28.5 %multiply_convert_fusion = bf16[4,4,512,1024]{3,2,1,0:T(8,128)(2,1)} fusion(f32[4,4,512,1024]{3,2,1,0:T(8,128)} %get-tuple-element.44, f32[4,4,512,1024]{3,2,1,0:T(8,128)} %get-tuple-element.38, f32[4,4,512]{2,1,0:T(4,128)S(1)} %get-tuple-element.43, f32[4,4,512]{2,1,0:T(4,128)S(1)} %bitcast.157), kind=kLoop, calls=%fused_computation | loop fusion | flops 41943040 | bytes 83951616 | tf_op jit(solution)/shard_map/convert_element_type | solution.py:218
  676.2 10.9 broadcast_multiply_fusion
  687.1 5.5 copy.50
  693.1 3.5 convolution_bitcast_fusion.1
  696.6 20.4 %fusion.22 = bf16[4,512,1024]{2,1,0:T(8,128)(2,1)S(1)} fusion(f32[4,512,1024]{2,1,0:T(8,128)} %copy-done.17, u8[512,1024]{1,0:T(8,128)(4,1)S(1)} %copy-done.31, u8[512,1024]{1,0:T(8,128)(4,1)S(1)} %copy-done.30), kind=kLoop, calls=%fused_computation.34 | loop fusion | flops 146800640 | bytes 13631488 | tf_op jit(solution)/shard_map/convert_element_type | solution.py:130
  717.0 1.8 convolution_convert_fusion.8
  720.2 6.2 convolution_convert_fusion
  726.7 11.0 multiply_convert_fusion.2
  739.1 1.7 convert_bitcast_fusion
  740.8 6.4 reduce-scatter.3.cloned.1.call-done
  747.2 1.7 convert_bitcast_fusion.1
  748.9 8.8 convolution_bitcast_fusion
  759.9 3.0 fusion.140
  764.3 72.5 %all-reduce.19.cloned.1.call-done = (bf16[4,512,1024]{2,1,0:T(8,128)(2,1)}, bf16[4,512,16]{1,2,0:T(8,128)(2,1)}) async-done(((bf16[4,512,1024]{2,1,0:T(8,128)(2,1)}, bf16[4,512,16]{1,2,0:T(8,128)(2,1)}), (bf16[4,512,1024]{2,1,0:T(8,128)(2,1)}, bf16[4,512,16]{1,2,0:T(8,128)(2,1)})) %all-reduce.19.cloned.1.call-update) | async-done | bytes 4259856 | tf_op jit(solution)/shard_map/psum | solution.py:136
  836.7 3.1 fusion.56
  839.9 2.8 convolution_bitcast_fusion.2
  844.8 2.6 fusion.71
  848.5 22.0 %all-reduce.22 = bf16[4,3,512,16]{2,3,1,0:T(8,128)(2,1)S(1)} all-reduce(f32[4,3,512,16]{2,3,1,0:T(8,128)S(1)} %fusion.99), channel_id=1, replica_groups=mesh['shard'=4,'context'=2,'tensor'=4] {'tensor'}, use_global_device_ids=true, to_apply=%region_18.0 | all-reduce | flops 98304 | bytes 589824 | tf_op jit(solution)/shard_map/psum | solution.py:255
  870.7 3.8 fusion.96
  877.0 2.8 fusion.62
  879.9 8.5 add_convert_fusion
  888.4 110.2 %all-reduce.15.cloned.1.call-done = f32[4,512,1024]{2,1,0:T(8,128)} async-done(((f32[4,512,1024]{2,1,0:T(8,128)}), f32[4,512,1024]{2,1,0:T(8,128)}) %all-reduce.15.cloned.1.call-update) | async-done | bytes 8388624 | tf_op jit(solution)/shard_map/psum | solution.py:255
  998.6 6.4 fusion.133
  1005.7 12.8 %fusion.17 = f32[4,512,1024]{2,1,0:T(8,128)} fusion(bf16[4,512,1024]{2,1,0:T(8,128)(2,1)S(1)} %copy-done.4, f32[4,512,1024]{2,1,0:T(8,128)S(1)} %get-tuple-element.45, f32[4,512]{1,0:T(4,128)S(1)} %broadcast_multiply_fusion.1, f32[4,512]{1,0:T(4,128)S(1)} %broadcast_multiply_fusion.2, f32[4,512]{1,0:T(4,128)S(1)} %copy-done.37, f32[4,512]{1,0:T(4,128)S(1)} %copy-done.33, ...), kind=kLoop, calls=%fused_computation.29 | loop fusion | flops 33554432 | bytes 42008576 | tf_op jit(solution)/shard_map/add | solution.py:263
  1018.5 154.7 %all-reduce.17.cloned.1.call-done = (f32[8,4,1024,16]{2,0,3,1:T(8,128)}, f32[8,3,16,256]{3,0,2,1:T(8,128)}, f32[8,16,1024]{2,0,1:T(8,128)}, f32[8,256,16]{1,0,2:...) async-done(((f32[8,4,1024,16]{2,0,3,1:T(8,128)}, f32[8,3,16,256]{3,0,2,1:T(8,128)}, f32[8,16,1024]{2,0,1:T(8,128)}, f32[8,256,16]{1,0,2:T(8,128)}, ...) | async-done | bytes 4718608 | tf_op jit(solution)/shard_map/psum | solution.py:270
  1173.2 4.1 copy.58
  1178.9 1.9 copy.59
  1180.8 2.1 copy.60
  1182.9 2.1 copy.62
  1185.0 2.8 copy.63
  (203 shorter events, 33.6 us)
Async XLA Ops:
  7.2 8.2 copy-start.52
  7.2 8.2 copy-start.44
  7.2 8.4 copy-start.57
  7.2 8.4 copy-start.68
  7.2 50.6 %all-gather.8.cloned.1.call-start = ((), (), s32[]{:S(2)}) async-start(), calls=%async_computation.2 | async-start | bytes 1769472 | tf_op jit(solution)/shard_map/all_gather | solution.py:69
  9.1 97.3 %all-gather.16.cloned.1.call-start = ((), (), s32[]{:S(2)}) async-start(), calls=%async_computation.11 | async-start | bytes 3145728 | tf_op jit(solution)/shard_map/all_gather | solution.py:93
  10.9 6.9 copy-start.20
  13.9 43.9 %copy-start.32 = (f32[4,512]{1,0:T(4,128)}, f32[4,512]{1,0:T(4,128)S(1)}, u32[]{:S(2)}) copy-start(f32[4,512]{1,0:T(4,128)S(1)} %broadcast_multiply_fusion.6) | copy-start | bytes 24580
  15.4 42.5 %copy-start.36 = (f32[4,512]{1,0:T(4,128)}, f32[4,512]{1,0:T(4,128)S(1)}, u32[]{:S(2)}) copy-start(f32[4,512]{1,0:T(4,128)S(1)} %add_rsqrt_fusion.1) | copy-start | bytes 24580
  15.7 48.3 %copy-start.34 = (bf16[4,3,16,256]{3,0,2,1:T(4,128)(2,1)}, bf16[4,3,16,256]{3,0,2,1:T(4,128)(2,1)S(1)}, u32[]{:S(2)}) copy-start(bf16[4,3,16,256]{3,0,2,1:T(4,128)(2,1)S(1)} %convolution_convert_fusion.6) | copy-start | bytes 294916
  17.8 46.1 %copy-start.45 = (bf16[4,3,16,512]{3,2,1,0:T(8,128)(2,1)}, bf16[4,3,16,512]{3,2,1,0:T(8,128)(2,1)S(1)}, u32[]{:S(2)}) copy-start(bf16[4,3,16,512]{3,2,1,0:T(8,128)(2,1)S(1)} %convolution_convert_fusion.3) | copy-start | bytes 589828
  66.7 55.5 %copy-start.15 = (bf16[4,1,512,256]{2,3,1,0:T(8,128)(2,1)}, bf16[4,1,512,256]{2,3,1,0:T(8,128)(2,1)S(1)}, u32[]{:S(2)}) copy-start(bf16[4,1,512,256]{2,3,1,0:T(8,128)(2,1)S(1)} %get-tuple-element.31) | copy-start | bytes 3145732
  66.7 74.4 %all-gather.14.cloned.1.call-start = ((), (), s32[]{:S(2)}) async-start(), calls=%async_computation.10 | async-start | bytes 3145728 | tf_op jit(solution)/shard_map/all_gather | solution.py:94
  67.5 124.8 %all-gather.12.cloned.1.call-start = ((), (), s32[]{:S(2)}) async-start(), calls=%async_computation.5 | async-start | bytes 2359296 | tf_op jit(solution)/shard_map/all_gather | solution.py:74
  68.0 280.6 %all-reduce.11.cloned.1.call-start = ((), (), s32[]{:S(2)}) async-start(), calls=%async_computation.3 | async-start | bytes 16777216 | tf_op jit(solution)/shard_map/psum | solution.py:115
  155.5 47.4 %copy-start.13 = (bf16[4,4,64,512]{3,2,1,0:T(8,128)(2,1)}, bf16[4,4,64,512]{3,2,1,0:T(8,128)(2,1)S(1)}, u32[]{:S(2)}) copy-start(bf16[4,4,64,512]{3,2,1,0:T(8,128)(2,1)S(1)} %fusion.55) | copy-start | bytes 3145732
  155.5 6.0 copy-start.64
  155.5 6.0 copy-start.56
  155.6 6.2 copy-start.41
  160.3 239.6 %all-gather.10.cloned.1.call-start = ((), (), s32[]{:S(2)}) async-start(), calls=%async_computation.4 | async-start | bytes 2359296 | tf_op jit(solution)/shard_map/all_gather | solution.py:73
  160.9 423.2 %all-reduce.13.cloned.1.call-start = ((), (), s32[]{:S(2)}) async-start(), calls=%async_computation.6 | async-start | bytes 16777216 | tf_op jit(solution)/shard_map/psum | solution.py:177
  161.5 41.3 %copy-start.60 = (f32[1,1024]{1,0:T(1,128)}, f32[1,1024]{1,0:T(1,128)S(1)}, u32[]{:S(2)}) copy-start(f32[1,1024]{1,0:T(1,128)S(1)} %get-tuple-element.35) | copy-start | bytes 12292
  163.9 39.0 %copy-start.27 = (bf16[4,16,1024]{2,0,1:T(4,128)(2,1)}, bf16[4,16,1024]{2,0,1:T(4,128)(2,1)S(1)}, u32[]{:S(2)}) copy-start(bf16[4,16,1024]{2,0,1:T(4,128)(2,1)S(1)} %get-tuple-element.33) | copy-start | bytes 393220
  167.3 245.0 %copy-start.47 = (bf16[4,512,16]{1,2,0:T(8,128)(2,1)}, bf16[4,512,16]{1,2,0:T(8,128)(2,1)S(1)}, u32[]{:S(2)}) copy-start(bf16[4,512,16]{1,2,0:T(8,128)(2,1)S(1)} %fusion.59) | copy-start | bytes 196612
  218.6 136.4 %copy-start.25 = (bf16[4,512,16]{1,2,0:T(8,128)(2,1)}, bf16[4,512,16]{1,2,0:T(8,128)(2,1)S(1)}, u32[]{:S(2)}) copy-start(bf16[4,512,16]{1,2,0:T(8,128)(2,1)S(1)} %all-reduce.20) | copy-start | bytes 196612
  355.1 236.5 %copy-start.38 = (f32[4,512]{1,0:T(4,128)}, f32[4,512]{1,0:T(4,128)S(1)}, u32[]{:S(2)}) copy-start(f32[4,512]{1,0:T(4,128)S(1)} %broadcast_multiply_fusion.5) | copy-start | bytes 24580
  356.3 235.3 %copy-start.42 = (f32[4,512]{1,0:T(4,128)}, f32[4,512]{1,0:T(4,128)S(1)}, u32[]{:S(2)}) copy-start(f32[4,512]{1,0:T(4,128)S(1)} %add_rsqrt_fusion) | copy-start | bytes 24580
  412.3 9.1 copy-start.17
  412.3 11.1 copy-start.67
  430.4 308.7 %reduce-scatter.5.cloned.1.call-start = ((), (), s32[]{:S(2)}) async-start(), calls=%async_computation.8 | async-start | bytes 6291456 | tf_op jit(solution)/shard_map/reduce_scatter | solution.py:239
  584.1 7.5 copy-start.9
  591.5 8.2 copy-start.5
  591.6 8.2 copy-start.48
  591.6 8.2 copy-start.50
  618.9 5.9 copy-start.19
  624.5 122.8 %reduce-scatter.3.cloned.1.call-start = ((), (), s32[]{:S(2)}) async-start(), calls=%async_computation.7 | async-start | bytes 6291456 | tf_op jit(solution)/shard_map/reduce_scatter | solution.py:236
  647.7 28.5 %copy-start.16 = (bf16[4,1,512,256]{2,3,1,0:T(8,128)(2,1)S(1)}, bf16[4,1,512,256]{2,3,1,0:T(8,128)(2,1)}, u32[]{:S(2)}) copy-start(bf16[4,1,512,256]{2,3,1,0:T(8,128)(2,1)} %copy-done.15) | copy-start | bytes 3145732
  687.1 9.5 copy-start.30
  687.1 9.5 copy-start.31
  692.6 144.2 %all-reduce.19.cloned.1.call-start = ((), (), s32[]{:S(2)}) async-start(), calls=%async_computation.13 | async-start | bytes 8519680 | tf_op jit(solution)/shard_map/psum | solution.py:136
  696.6 22.2 %copy-start.12 = (bf16[4,512,1024]{2,1,0:T(8,128)(2,1)S(1)}, bf16[4,512,1024]{2,1,0:T(8,128)(2,1)}, u32[]{:S(2)}) copy-start(bf16[4,512,1024]{2,1,0:T(8,128)(2,1)} %copy-done.11) | copy-start | bytes 12582916
  720.2 6.5 copy-start.18
  726.5 272.1 %all-reduce.15.cloned.1.call-start = ((), (), s32[]{:S(2)}) async-start(), calls=%async_computation.9 | async-start | bytes 16777216 | tf_op jit(solution)/shard_map/psum | solution.py:255
  757.7 79.1 %copy-start.61 = (f32[1,1024]{1,0:T(1,128)S(1)}, f32[1,1024]{1,0:T(1,128)}, u32[]{:S(2)}) copy-start(f32[1,1024]{1,0:T(1,128)} %copy-done.60) | copy-start | bytes 12292
  757.7 82.2 %copy-start.26 = (bf16[4,512,16]{1,2,0:T(8,128)(2,1)S(1)}, bf16[4,512,16]{1,2,0:T(8,128)(2,1)}, u32[]{:S(2)}) copy-start(bf16[4,512,16]{1,2,0:T(8,128)(2,1)} %copy-done.25) | copy-start | bytes 196612
  757.7 415.5 %all-reduce.17.cloned.1.call-start = ((), (), s32[]{:S(2)}) async-start(), calls=%async_computation.12 | async-start | bytes 9437184 | tf_op jit(solution)/shard_map/psum | solution.py:270
  759.9 82.9 %copy-start.14 = (bf16[4,4,64,512]{3,2,1,0:T(8,128)(2,1)S(1)}, bf16[4,4,64,512]{3,2,1,0:T(8,128)(2,1)}, u32[]{:S(2)}) copy-start(bf16[4,4,64,512]{3,2,1,0:T(8,128)(2,1)} %copy-done.13) | copy-start | bytes 3145732
  836.7 10.8 copy-start.23
  836.7 10.8 copy-start.35
  842.8 27.8 %copy-start.33 = (f32[4,512]{1,0:T(4,128)S(1)}, f32[4,512]{1,0:T(4,128)}, u32[]{:S(2)}) copy-start(f32[4,512]{1,0:T(4,128)} %copy-done.32) | copy-start | bytes 24580
  842.8 27.8 %copy-start.37 = (f32[4,512]{1,0:T(4,128)S(1)}, f32[4,512]{1,0:T(4,128)}, u32[]{:S(2)}) copy-start(f32[4,512]{1,0:T(4,128)} %copy-done.36) | copy-start | bytes 24580
  843.2 27.4 %copy-start.58 = (f32[1024]{0:T(1024)S(1)}, f32[1024]{0:T(1024)}, u32[]{:S(2)}) copy-start(f32[1024]{0:T(1024)} %param.21) | copy-start | bytes 12292
  843.2 27.4 %copy-start.69 = (f32[1024]{0:T(1024)S(1)}, f32[1024]{0:T(1024)}, u32[]{:S(2)}) copy-start(f32[1024]{0:T(1024)} %param.22) | copy-start | bytes 12292
  870.6 5.1 copy-start.54
  875.0 4.8 copy-start.28
  879.9 118.7 %copy-start.21 = (bf16[4,3,1024,16]{2,0,3,1:T(4,128)(2,1)S(1)}, bf16[4,3,1024,16]{2,0,3,1:T(4,128)(2,1)}, u32[]{:S(2)}) copy-start(bf16[4,3,1024,16]{2,0,3,1:T(4,128)(2,1)} %copy-done.20) | copy-start | bytes 1179652
  879.9 118.7 %copy-start.59 = (f32[1024]{0:T(1024)S(1)}, f32[1024]{0:T(1024)}, u32[]{:S(2)}) copy-start(f32[1024]{0:T(1024)} %param.21) | copy-start | bytes 12292
  888.4 116.6 %copy-start.39 = (f32[4,512]{1,0:T(4,128)S(1)}, f32[4,512]{1,0:T(4,128)}, u32[]{:S(2)}) copy-start(f32[4,512]{1,0:T(4,128)} %copy-done.38) | copy-start | bytes 24580
  888.4 116.6 %copy-start.43 = (f32[4,512]{1,0:T(4,128)S(1)}, f32[4,512]{1,0:T(4,128)}, u32[]{:S(2)}) copy-start(f32[4,512]{1,0:T(4,128)} %copy-done.42) | copy-start | bytes 24580
  888.4 116.6 %copy-start.49 = (f32[4,512]{1,0:T(4,128)S(1)}, f32[4,512]{1,0:T(4,128)}, u32[]{:S(2)}) copy-start(f32[4,512]{1,0:T(4,128)} %copy-done.48) | copy-start | bytes 24580
  888.4 116.6 %copy-start.51 = (f32[4,512]{1,0:T(4,128)S(1)}, f32[4,512]{1,0:T(4,128)}, u32[]{:S(2)}) copy-start(f32[4,512]{1,0:T(4,128)} %copy-done.50) | copy-start | bytes 24580
  998.6 6.5 copy-start.4
  998.6 7.1 copy-start.10
  1005.7 182.2 %copy-start.1 = (bf16[8,4,1024,16]{2,3,1,0:T(8,128)(2,1)S(1)}, bf16[8,4,1024,16]{2,3,1,0:T(8,128)(2,1)}, u32[]{:S(2)}) copy-start(bf16[8,4,1024,16]{2,3,1,0:T(8,128)(2,1)} %param.30) | copy-start | bytes 3145732
  (18 other events, 51.8 us)
Sparse Core Ops, SparseCore 0:
  10.7 47.1 all-gather.7
  66.8 39.5 all-gather.15
  108.6 32.5 all-gather.13
  143.1 49.0 all-gather.11
  195.1 153.4 all-reduce.10
  350.6 49.2 all-gather.9
  430.5 153.5 all-reduce.12
  624.6 54.5 reduce-scatter.4
  692.7 54.4 reduce-scatter.2
  750.1 86.5 all-reduce.18
  839.2 159.3 all-reduce.14
  1003.2 169.8 all-reduce.16
where the time goes:
time: 1200 us; the launch traced here: 1190 us
  waiting for transfers between devices  724 us (60%)
  matrix products  234 us (20%)
  other arithmetic  94.5 us (8%)
  blocking collectives  85.1 us (7%)
  local copies, waits for them, and re-layouts  39.2 us (3%)
  between operations  15.4 us (1%)
    psum x1, waiting for transfers between devices, per_device(): lax.psum((down_total, qkv_up_total, fc1_up_total, proj_down_total, fc2_do...  155 us
    psum x1, waiting for transfers between devices, per_device(): lax.psum((normed_two_part, fc1_rank_part), 'tensor')  135 us
    psum x1, waiting for transfers between devices, per_device(): lax.psum((proj_part, proj_rank_part), 'tensor')  130 us
    psum x1, waiting for transfers between devices, per_device(): grad_normed, grad_rank_total = lax.psum((normed_part, rank_part), 'tensor')  110 us
    psum x1, waiting for transfers between devices, per_device(): lax.psum(mlp_part.astype(jnp.bfloat16), 'tensor').astype(jnp.float32)  72.5 us
    all_gather x1, waiting for transfers between devices, per_device(): lax.all_gather(w_qkv, ('shard', 'context'), axis=0, tiled=True)  40 us
    all_gather x1, waiting for transfers between devices, per_device(): lax.all_gather(w_fc1, ('shard', 'context'), axis=0, tiled=True)  38.2 us
    all_gather x1, blocking collectives, per_device(): lax.all_gather(w_proj, ('shard', 'context'), axis=0, tiled=True)  32.2 us
  transfers between devices with their start and end apart: 12, of which 11 were waited for; matrix products, arithmetic and copies ran while one was open for 22% of the time, Pallas kernels for 0%

commit v1 on v0

--- a/solution.py
+++ b/solution.py
@@ -133,7 +133,9 @@
         "ilf,ifr->ilr", activation, sel_fc2, preferred_element_type=jnp.float32
     )
     mlp_total, fc2_rank_total = (
-        lax.psum(mlp_part.astype(jnp.bfloat16), "tensor").astype(jnp.float32),
+        jnp.sum(lax.all_gather(mlp_part.astype(jnp.bfloat16), "tensor"), axis=0).astype(
+            jnp.float32
+        ),
         lax.psum(fc2_rank_part.astype(jnp.bfloat16), "tensor").astype(jnp.float32),
     )
     fc2_rank = fc2_rank_total.astype(jnp.bfloat16)

time: 1200 us -> 1260 us (1.050)
  waiting for transfers between devices: 724 us -> 766 us
    all_gather x0 -> x1, waiting for transfers between devices: none -> 91.3 us  [per_device(): lax.all_gather(mlp_part.astype(jnp.bfloat16), 'tensor')]
    psum x1, waiting for transfers between devices: 72.5 us -> 16.7 us  [per_device(): lax.psum(fc2_rank_part.astype(jnp.bfloat16), 'tensor').astype(jnp.float32)]
    unnamed x147 -> x139, local copies, waits for them, and re-layouts: 24.2 us -> 26.1 us
  transfers between devices with their start and end apart: 12 -> 13, of which waited for: 11 -> 12; matrix products, arithmetic and copies ran while one was open for 22% -> 22% of each run, Pallas kernels for 0% -> 0%
where the time goes in v1:
time: 1260 us; the launch traced here: 1250 us
  waiting for transfers between devices  766 us (61%)
  matrix products  238 us (19%)
  other arithmetic  106 us (8%)
  blocking collectives  84.6 us (7%)
  local copies, waits for them, and re-layouts  41 us (3%)
  between operations  15 us (1%)
    psum x1, waiting for transfers between devices, per_device(): lax.psum((down_total, qkv_up_total, fc1_up_total, proj_down_total, fc2_do...  155 us
    psum x1, waiting for transfers between devices, per_device(): lax.psum((normed_two_part, fc1_rank_part), 'tensor')  134 us
    psum x1, waiting for transfers between devices, per_device(): lax.psum((proj_part, proj_rank_part), 'tensor')  130 us
    psum x1, waiting for transfers between devices, per_device(): grad_normed, grad_rank_total = lax.psum((normed_part, rank_part), 'tensor')  113 us
    all_gather x1, waiting for transfers between devices, per_device(): lax.all_gather(mlp_part.astype(jnp.bfloat16), 'tensor')  91.3 us
    all_gather x1, waiting for transfers between devices, per_device(): lax.all_gather(w_qkv, ('shard', 'context'), axis=0, tiled=True)  40 us
    all_gather x1, waiting for transfers between devices, per_device(): lax.all_gather(w_fc1, ('shard', 'context'), axis=0, tiled=True)  38.3 us
    all_gather x1, blocking collectives, per_device(): lax.all_gather(w_proj, ('shard', 'context'), axis=0, tiled=True)  32.4 us
  transfers between devices with their start and end apart: 13, of which 12 were waited for; matrix products, arithmetic and copies ran while one was open for 22% of the time, Pallas kernels for 0%

profile of v1, /device:TPU:0, one launch (start us, length us, event | category | flops | bytes accessed | tf_op | source)
XLA Modules:
  0.0 1251.9 jit_solution(9301459188650260766)
XLA Ops:
  10.9 3.0 convert_reduce_fusion
  15.7 2.1 convolution_convert_fusion.3
  17.8 40.0 %all-gather.10.cloned.1.call-done = bf16[1024,3,256]{0,2,1:T(8,128)(2,1)} async-done(((bf16[128,3,256]{0,2,1:T(8,128)(2,1)}), bf16[1024,3,256]{0,2,1:T(8,128)(2,1)}) %all-gather.10.cloned.1.call-update) | async-done | bytes 1572880 | tf_op jit(solution)/shard_map/all_gather | solution.py:69
  57.8 6.1 fusion.53
  68.1 32.4 %all_gather.31 = bf16[1024,256]{1,0:T(8,128)(2,1)S(1)} all-gather(bf16[128,256]{1,0:T(8,128)(2,1)S(1)} %copy-done.51), channel_id=1, replica_groups=mesh['shard'=4,'context'=2,'tensor'=4] {'shard','context'}, dimensions={0}, use_global_device_ids=true | all-gather | bytes 589824 | tf_op jit(solution)/shard_map/all_gather | solution.py:70
  100.5 6.1 all-gather.18.cloned.1.call-done
  106.6 15.7 %multiply_reduce_fusion.1 = (f32[4,4,512]{2,1,0:T(4,128)S(1)}, f32[4,4,512,1024]{3,2,1,0:T(8,128)}) fusion(bf16[4,512,4,64]{1,3,2,0:T(8,128)(2,1)S(1)} %bitcast.149, bf16[4,1024,4,64]{1,3,2,0:T(8,128)(2,1)} %bitcast.151), kind=kOutput, calls=%fused_computation.6 | convolution fusion | flops 1090510848 | bytes 36732928 | tf_op jit(solution)/shard_map/iqhe,ikhe->ihqk/dot_general | solution.py:99
  122.3 14.2 %fusion = f32[4,4,512]{2,1,0:T(4,128)S(1)} fusion(f32[4,4,512,1024]{3,2,1,0:T(8,128)} %get-tuple-element.44, f32[4,4,512]{2,1,0:T(4,128)S(1)} %get-tuple-element.43), kind=kLoop, calls=%fused_computation.5 | loop fusion | flops 25157632 | bytes 33619968 | tf_op jit(solution)/shard_map/reduce_sum | solution.py:104
  136.5 4.8 all-gather.16.cloned.1.call-done
  141.3 14.4 %fusion.55 = bf16[4,4,64,512]{3,2,1,0:T(8,128)(2,1)S(1)} fusion(bf16[4,1024,4,64]{1,3,2,0:T(8,128)(2,1)} %bitcast.155, f32[4,4,512,1024]{3,2,1,0:T(8,128)} %get-tuple-element.44, f32[4,4,512]{2,1,0:T(4,128)S(1)} %fusion, f32[4,4,512]{2,1,0:T(4,128)S(1)} %get-tuple-element.43), kind=kOutput, calls=%fused_computation.92 | convolution fusion | flops 1107820544 | bytes 36765696 | tf_op jit(solution)/shard_map/ihqk,ikhe->iqhe/dot_general | solution.py:107
  155.8 4.7 fusion.69
  163.8 3.4 fusion.59
  167.2 25.2 %all-gather.14.cloned.1.call-done = bf16[1024,1024]{1,0:T(8,128)(2,1)} async-done(((bf16[128,1024]{1,0:T(8,128)(2,1)}), bf16[1024,1024]{1,0:T(8,128)(2,1)}) %all-gather.14.cloned.1.call-update) | async-done | bytes 2097168 | tf_op jit(solution)/shard_map/all_gather | solution.py:74
  192.4 10.6 fusion.42
  203.3 15.5 %all-reduce.19 = bf16[4,512,16]{1,2,0:T(8,128)(2,1)S(1)} all-reduce(f32[4,512,16]{1,2,0:T(8,128)S(1)} %fusion.110), channel_id=1, replica_groups=mesh['shard'=4,'context'=2,'tensor'=4] {'tensor'}, use_global_device_ids=true, to_apply=%region_5.0 | all-reduce | flops 32768 | bytes 196608 | tf_op jit(solution)/shard_map/psum | solution.py:115
  218.9 130.0 %all-reduce.10.cloned.1.call-done = f32[4,512,1024]{2,1,0:T(8,128)} async-done(((f32[4,512,1024]{2,1,0:T(8,128)}), f32[4,512,1024]{2,1,0:T(8,128)}) %all-reduce.10.cloned.1.call-update) | async-done | bytes 8388624 | tf_op jit(solution)/shard_map/psum | solution.py:115
  348.9 6.4 fusion.137
  358.6 2.0 copy-done.7
  361.8 38.3 %all-gather.12.cloned.1.call-done = bf16[1024,1024]{1,0:T(8,128)(2,1)} async-done(((bf16[128,1024]{1,0:T(8,128)(2,1)}), bf16[1024,1024]{1,0:T(8,128)(2,1)}) %all-gather.12.cloned.1.call-update) | async-done | bytes 2097168 | tf_op jit(solution)/shard_map/all_gather | solution.py:73
  400.1 6.9 fusion.48
  407.0 5.6 fusion.51
  412.6 9.0 fusion.28
  421.7 2.0 copy-done.11
  423.7 6.9 fusion.46
  431.2 3.4 fusion.89
  434.5 15.3 %all-reduce.20 = bf16[4,512,16]{1,2,0:T(8,128)(2,1)S(1)} all-reduce(f32[4,512,16]{1,2,0:T(8,128)S(1)} %fusion.89), channel_id=1, replica_groups=mesh['shard'=4,'context'=2,'tensor'=4] {'tensor'}, use_global_device_ids=true, to_apply=%region_11.0 | all-reduce | flops 32768 | bytes 196608 | tf_op jit(solution)/shard_map/psum | solution.py:179
  449.9 134.4 %all-reduce.14.cloned.1.call-done = f32[4,512,1024]{2,1,0:T(8,128)} async-done(((f32[4,512,1024]{2,1,0:T(8,128)}), f32[4,512,1024]{2,1,0:T(8,128)}) %all-reduce.14.cloned.1.call-update) | async-done | bytes 8388624 | tf_op jit(solution)/shard_map/psum | solution.py:179
  584.3 7.4 fusion.134
  592.5 7.4 multiply_convert_fusion.1
  603.7 15.3 %fusion.2 = f32[4,4,64,1024]{3,2,1,0:T(8,128)} fusion(bf16[4,512,4,64]{1,3,2,0:T(8,128)(2,1)S(1)} %bitcast.147, f32[4,4,512,1024]{3,2,1,0:T(8,128)} %get-tuple-element.44, f32[4,4,512]{2,1,0:T(4,128)S(1)} %bitcast.157), kind=kOutput, calls=%fused_computation.8 | convolution fusion | flops 1098907648 | bytes 38830080 | tf_op jit(solution)/shard_map/ihqk,iqhe->ikhe/dot_general | solution.py:231
  619.0 5.5 copy.89
  624.8 22.9 %multiply_reduce_fusion = (f32[4,4,512]{2,1,0:T(4,128)S(1)}, f32[4,4,512,1024]{3,2,1,0:T(8,128)}) fusion(f32[4,4,512,1024]{3,2,1,0:T(8,128)} %get-tuple-element.44, f32[4,4,512]{2,1,0:T(4,128)S(1)} %bitcast.158, bf16[4,512,4,64]{1,3,2,0:T(8,128)(2,1)S(1)} %bitcast.148, bf16[4,1024,4,64]{1,3,2,0:T(8,128)(2,1)S(1)} %bitcast.156), kind=kOutput, calls=%fused_computation.1 | convolution fusion | flops 1107288064 | bytes 70320128 | tf_op jit(solution)/shard_map/iqhe,ikhe->ihqk/dot_general | solution.py:216
  647.7 28.5 %multiply_convert_fusion = bf16[4,4,512,1024]{3,2,1,0:T(8,128)(2,1)} fusion(f32[4,4,512,1024]{3,2,1,0:T(8,128)} %get-tuple-element.50, f32[4,4,512,1024]{3,2,1,0:T(8,128)} %get-tuple-element.44, f32[4,4,512]{2,1,0:T(4,128)S(1)} %get-tuple-element.49, f32[4,4,512]{2,1,0:T(4,128)S(1)} %bitcast.159), kind=kLoop, calls=%fused_computation | loop fusion | flops 41943040 | bytes 83951616 | tf_op jit(solution)/shard_map/convert_element_type | solution.py:220
  676.2 10.9 broadcast_multiply_fusion
  687.1 5.5 copy.88
  692.7 3.6 convolution_bitcast_fusion.1
  696.2 20.2 %fusion.22 = bf16[4,512,1024]{2,1,0:T(8,128)(2,1)S(1)} fusion(f32[4,512,1024]{2,1,0:T(8,128)} %copy-done.16, u8[512,1024]{1,0:T(8,128)(4,1)S(1)} %copy-done.30, u8[512,1024]{1,0:T(8,128)(4,1)S(1)} %copy-done.29), kind=kLoop, calls=%fused_computation.34 | loop fusion | flops 146800640 | bytes 13631488 | tf_op jit(solution)/shard_map/convert_element_type | solution.py:130
  716.5 2.0 copy-done.6
  720.3 2.8 fusion.138
  723.4 11.2 multiply_convert_fusion.2
  737.7 9.5 reduce-scatter.3.cloned.1.call-done
  748.9 8.6 convolution_bitcast_fusion
  759.7 3.0 fusion.140
  762.7 2.1 fusion.76
  764.8 16.7 %all-reduce.12.cloned.1.call-done = bf16[4,512,16]{1,2,0:T(8,128)(2,1)} async-done(((bf16[4,512,16]{1,2,0:T(8,128)(2,1)}), bf16[4,512,16]{1,2,0:T(8,128)(2,1)}) %all-reduce.12.cloned.1.call-update) | async-done | bytes 65552 | tf_op jit(solution)/shard_map/psum | solution.py:139
  781.5 3.1 fusion.56
  784.6 2.8 convolution_bitcast_fusion.2
  788.9 2.0 fusion.71
  792.0 21.3 %all-reduce.21 = bf16[4,3,512,16]{2,3,1,0:T(8,128)(2,1)S(1)} all-reduce(f32[4,3,512,16]{2,3,1,0:T(8,128)S(1)} %fusion.99), channel_id=1, replica_groups=mesh['shard'=4,'context'=2,'tensor'=4] {'tensor'}, use_global_device_ids=true, to_apply=%region_18.0 | all-reduce | flops 98304 | bytes 589824 | tf_op jit(solution)/shard_map/psum | solution.py:257
  813.4 3.8 fusion.96
  819.7 2.8 fusion.62
  822.8 8.4 convolution_convert_fusion
  831.2 112.7 %all-reduce.16.cloned.1.call-done = f32[4,512,1024]{2,1,0:T(8,128)} async-done(((f32[4,512,1024]{2,1,0:T(8,128)}), f32[4,512,1024]{2,1,0:T(8,128)}) %all-reduce.16.cloned.1.call-update) | async-done | bytes 8388624 | tf_op jit(solution)/shard_map/psum | solution.py:257
  943.9 6.4 fusion.133
  951.0 12.7 %fusion.17 = f32[4,512,1024]{2,1,0:T(8,128)} fusion(bf16[4,512,1024]{2,1,0:T(8,128)(2,1)S(1)} %copy-done.4, f32[4,512,1024]{2,1,0:T(8,128)S(1)} %get-tuple-element.51, f32[4,512]{1,0:T(4,128)S(1)} %broadcast_multiply_fusion.1, f32[4,512]{1,0:T(4,128)S(1)} %broadcast_multiply_fusion.2, f32[4,512]{1,0:T(4,128)S(1)} %copy-done.36, f32[4,512]{1,0:T(4,128)S(1)} %copy-done.32, ...), kind=kLoop, calls=%fused_computation.29 | loop fusion | flops 33554432 | bytes 42008576 | tf_op jit(solution)/shard_map/add | solution.py:265
  963.7 154.7 %all-reduce.18.cloned.1.call-done = (f32[8,4,1024,16]{2,0,3,1:T(8,128)}, f32[8,3,16,256]{3,0,2,1:T(8,128)}, f32[8,16,1024]{2,0,1:T(8,128)}, f32[8,256,16]{1,0,2:...) async-done(((f32[8,4,1024,16]{2,0,3,1:T(8,128)}, f32[8,3,16,256]{3,0,2,1:T(8,128)}, f32[8,16,1024]{2,0,1:T(8,128)}, f32[8,256,16]{1,0,2:T(8,128)}, ...) | async-done | bytes 4718608 | tf_op jit(solution)/shard_map/psum | solution.py:272
  1118.4 4.1 copy.96
  1124.2 1.9 copy.97
  1126.1 2.2 copy.98
  1128.3 2.2 copy.100
  1130.5 3.0 copy.101
  1133.5 91.3 %all-gather.20.cloned.1.call-done = bf16[16,512,1024]{2,1,0:T(8,128)(2,1)} async-done(((bf16[4,512,1024]{2,1,0:T(8,128)(2,1)}), bf16[16,512,1024]{2,1,0:T(8,128)(2,1)}) %all-gather.20.cloned.1.call-update) | async-done | bytes 16777232 | tf_op jit(solution)/shard_map/all_gather | solution.py:136
  1224.8 12.1 reduce_sum.107
  1237.0 8.2 add_convert_fusion
  (199 shorter events, 39.1 us)
Async XLA Ops:
  7.2 8.2 copy-start.47
  7.2 8.2 copy-start.39
  7.2 8.4 copy-start.53
  7.2 8.4 copy-start.64
  7.2 50.6 %all-gather.10.cloned.1.call-start = ((), (), s32[]{:S(2)}) async-start(), calls=%async_computation.2 | async-start | bytes 1769472 | tf_op jit(solution)/shard_map/all_gather | solution.py:69
  9.1 97.5 %all-gather.18.cloned.1.call-start = ((), (), s32[]{:S(2)}) async-start(), calls=%async_computation.12 | async-start | bytes 3145728 | tf_op jit(solution)/shard_map/all_gather | solution.py:93
  9.2 4.7 copy-start.3
  10.9 6.9 copy-start.19
  13.9 43.9 %copy-start.31 = (f32[4,512]{1,0:T(4,128)}, f32[4,512]{1,0:T(4,128)S(1)}, u32[]{:S(2)}) copy-start(f32[4,512]{1,0:T(4,128)S(1)} %broadcast_multiply_fusion.6) | copy-start | bytes 24580
  15.4 42.5 %copy-start.35 = (f32[4,512]{1,0:T(4,128)}, f32[4,512]{1,0:T(4,128)S(1)}, u32[]{:S(2)}) copy-start(f32[4,512]{1,0:T(4,128)S(1)} %add_rsqrt_fusion.1) | copy-start | bytes 24580
  15.7 48.3 %copy-start.33 = (bf16[4,3,16,256]{3,0,2,1:T(4,128)(2,1)}, bf16[4,3,16,256]{3,0,2,1:T(4,128)(2,1)S(1)}, u32[]{:S(2)}) copy-start(bf16[4,3,16,256]{3,0,2,1:T(4,128)(2,1)S(1)} %convolution_convert_fusion.6) | copy-start | bytes 294916
  17.8 46.1 %copy-start.40 = (bf16[4,3,16,512]{3,2,1,0:T(8,128)(2,1)}, bf16[4,3,16,512]{3,2,1,0:T(8,128)(2,1)S(1)}, u32[]{:S(2)}) copy-start(bf16[4,3,16,512]{3,2,1,0:T(8,128)(2,1)S(1)} %convolution_convert_fusion.3) | copy-start | bytes 589828
  66.7 55.6 %copy-start.14 = (bf16[4,1,512,256]{2,3,1,0:T(8,128)(2,1)}, bf16[4,1,512,256]{2,3,1,0:T(8,128)(2,1)S(1)}, u32[]{:S(2)}) copy-start(bf16[4,1,512,256]{2,3,1,0:T(8,128)(2,1)S(1)} %get-tuple-element.37) | copy-start | bytes 3145732
  66.7 74.6 %all-gather.16.cloned.1.call-start = ((), (), s32[]{:S(2)}) async-start(), calls=%async_computation.11 | async-start | bytes 3145728 | tf_op jit(solution)/shard_map/all_gather | solution.py:94
  67.5 125.0 %all-gather.14.cloned.1.call-start = ((), (), s32[]{:S(2)}) async-start(), calls=%async_computation.5 | async-start | bytes 2359296 | tf_op jit(solution)/shard_map/all_gather | solution.py:74
  68.0 280.8 %all-reduce.10.cloned.1.call-start = ((), (), s32[]{:S(2)}) async-start(), calls=%async_computation.3 | async-start | bytes 16777216 | tf_op jit(solution)/shard_map/psum | solution.py:115
  155.7 47.4 %copy-start.12 = (bf16[4,4,64,512]{3,2,1,0:T(8,128)(2,1)}, bf16[4,4,64,512]{3,2,1,0:T(8,128)(2,1)S(1)}, u32[]{:S(2)}) copy-start(bf16[4,4,64,512]{3,2,1,0:T(8,128)(2,1)S(1)} %fusion.55) | copy-start | bytes 3145732
  155.7 5.6 copy-start.60
  155.8 5.6 copy-start.52
  155.8 5.9 copy-start.38
  160.5 239.6 %all-gather.12.cloned.1.call-start = ((), (), s32[]{:S(2)}) async-start(), calls=%async_computation.4 | async-start | bytes 2359296 | tf_op jit(solution)/shard_map/all_gather | solution.py:73
  161.1 423.2 %all-reduce.14.cloned.1.call-start = ((), (), s32[]{:S(2)}) async-start(), calls=%async_computation.7 | async-start | bytes 16777216 | tf_op jit(solution)/shard_map/psum | solution.py:179
  161.4 41.7 %copy-start.55 = (f32[1,1024]{1,0:T(1,128)}, f32[1,1024]{1,0:T(1,128)S(1)}, u32[]{:S(2)}) copy-start(f32[1,1024]{1,0:T(1,128)S(1)} %get-tuple-element.41) | copy-start | bytes 12292
  161.4 187.5 %copy-start.57 = (f32[1,1024]{1,0:T(1,128)}, f32[1,1024]{1,0:T(1,128)S(1)}, u32[]{:S(2)}) copy-start(f32[1,1024]{1,0:T(1,128)S(1)} %get-tuple-element.42) | copy-start | bytes 12292
  163.8 39.3 %copy-start.26 = (bf16[4,16,1024]{2,0,1:T(4,128)(2,1)}, bf16[4,16,1024]{2,0,1:T(4,128)(2,1)S(1)}, u32[]{:S(2)}) copy-start(bf16[4,16,1024]{2,0,1:T(4,128)(2,1)S(1)} %get-tuple-element.39) | copy-start | bytes 393220
  167.2 245.4 %copy-start.42 = (bf16[4,512,16]{1,2,0:T(8,128)(2,1)}, bf16[4,512,16]{1,2,0:T(8,128)(2,1)S(1)}, u32[]{:S(2)}) copy-start(bf16[4,512,16]{1,2,0:T(8,128)(2,1)S(1)} %fusion.59) | copy-start | bytes 196612
  218.9 136.4 %copy-start.24 = (bf16[4,512,16]{1,2,0:T(8,128)(2,1)}, bf16[4,512,16]{1,2,0:T(8,128)(2,1)S(1)}, u32[]{:S(2)}) copy-start(bf16[4,512,16]{1,2,0:T(8,128)(2,1)S(1)} %all-reduce.19) | copy-start | bytes 196612
  412.6 9.1 copy-start.16
  412.6 11.1 copy-start.63
  430.7 305.3 %reduce-scatter.5.cloned.1.call-start = ((), (), s32[]{:S(2)}) async-start(), calls=%async_computation.9 | async-start | bytes 6291456 | tf_op jit(solution)/shard_map/reduce_scatter | solution.py:241
  449.9 142.6 %copy-start.58 = (f32[1,1024]{1,0:T(1,128)S(1)}, f32[1,1024]{1,0:T(1,128)}, u32[]{:S(2)}) copy-start(f32[1,1024]{1,0:T(1,128)} %copy-done.57) | copy-start | bytes 12292
  584.3 8.2 copy-start.9
  591.8 8.1 copy-start.5
  619.0 5.8 copy-start.18
  624.5 122.7 %reduce-scatter.3.cloned.1.call-start = ((), (), s32[]{:S(2)}) async-start(), calls=%async_computation.8 | async-start | bytes 6291456 | tf_op jit(solution)/shard_map/reduce_scatter | solution.py:238
  647.7 28.5 %copy-start.15 = (bf16[4,1,512,256]{2,3,1,0:T(8,128)(2,1)S(1)}, bf16[4,1,512,256]{2,3,1,0:T(8,128)(2,1)}, u32[]{:S(2)}) copy-start(bf16[4,1,512,256]{2,3,1,0:T(8,128)(2,1)} %copy-done.14) | copy-start | bytes 3145732
  687.1 9.1 copy-start.29
  687.1 9.1 copy-start.30
  692.6 88.9 %all-reduce.12.cloned.1.call-start = ((), (), s32[]{:S(2)}) async-start(), calls=%async_computation.6 | async-start | bytes 131072 | tf_op jit(solution)/shard_map/psum | solution.py:139
  718.5 5.0 copy-start.17
  723.2 220.7 %all-reduce.16.cloned.1.call-start = ((), (), s32[]{:S(2)}) async-start(), calls=%async_computation.10 | async-start | bytes 16777216 | tf_op jit(solution)/shard_map/psum | solution.py:257
  757.5 27.1 %copy-start.25 = (bf16[4,512,16]{1,2,0:T(8,128)(2,1)S(1)}, bf16[4,512,16]{1,2,0:T(8,128)(2,1)}, u32[]{:S(2)}) copy-start(bf16[4,512,16]{1,2,0:T(8,128)(2,1)} %copy-done.24) | copy-start | bytes 196612
  757.5 360.9 %all-reduce.18.cloned.1.call-start = ((), (), s32[]{:S(2)}) async-start(), calls=%async_computation.14 | async-start | bytes 9437184 | tf_op jit(solution)/shard_map/psum | solution.py:272
  759.7 27.8 %copy-start.13 = (bf16[4,4,64,512]{3,2,1,0:T(8,128)(2,1)S(1)}, bf16[4,4,64,512]{3,2,1,0:T(8,128)(2,1)}, u32[]{:S(2)}) copy-start(bf16[4,4,64,512]{3,2,1,0:T(8,128)(2,1)} %copy-done.12) | copy-start | bytes 3145732
  781.5 6.4 copy-start.49
  781.5 9.4 copy-start.22
  781.5 9.4 copy-start.34
  787.5 25.8 %copy-start.32 = (f32[4,512]{1,0:T(4,128)S(1)}, f32[4,512]{1,0:T(4,128)}, u32[]{:S(2)}) copy-start(f32[4,512]{1,0:T(4,128)} %copy-done.31) | copy-start | bytes 24580
  787.5 25.8 %copy-start.36 = (f32[4,512]{1,0:T(4,128)S(1)}, f32[4,512]{1,0:T(4,128)}, u32[]{:S(2)}) copy-start(f32[4,512]{1,0:T(4,128)} %copy-done.35) | copy-start | bytes 24580
  787.6 25.8 %copy-start.54 = (f32[1024]{0:T(1024)S(1)}, f32[1024]{0:T(1024)}, u32[]{:S(2)}) copy-start(f32[1024]{0:T(1024)} %param.21) | copy-start | bytes 12292
  787.6 25.8 %copy-start.65 = (f32[1024]{0:T(1024)S(1)}, f32[1024]{0:T(1024)}, u32[]{:S(2)}) copy-start(f32[1024]{0:T(1024)} %param.22) | copy-start | bytes 12292
  813.4 4.4 copy-start.23
  813.4 4.4 copy-start.41
  813.4 5.1 copy-start.50
  822.5 121.3 %copy-start.20 = (bf16[4,3,1024,16]{2,0,3,1:T(4,128)(2,1)S(1)}, bf16[4,3,1024,16]{2,0,3,1:T(4,128)(2,1)}, u32[]{:S(2)}) copy-start(bf16[4,3,1024,16]{2,0,3,1:T(4,128)(2,1)} %copy-done.19) | copy-start | bytes 1179652
  822.5 402.3 %all-gather.20.cloned.1.call-start = ((), (), s32[]{:S(2)}) async-start(), calls=%async_computation.13 | async-start | bytes 20971520 | tf_op jit(solution)/shard_map/all_gather | solution.py:136
  831.2 119.1 %copy-start.44 = (f32[4,512]{1,0:T(4,128)S(1)}, f32[4,512]{1,0:T(4,128)}, u32[]{:S(2)}) copy-start(f32[4,512]{1,0:T(4,128)} %copy-done.43) | copy-start | bytes 24580
  831.2 119.1 %copy-start.46 = (f32[4,512]{1,0:T(4,128)S(1)}, f32[4,512]{1,0:T(4,128)}, u32[]{:S(2)}) copy-start(f32[4,512]{1,0:T(4,128)} %copy-done.45) | copy-start | bytes 24580
  943.9 6.4 copy-start.4
  943.9 7.1 copy-start.10
  1224.8 12.2 copy-start.27
  1224.8 12.2 copy-start.37
  1224.8 12.2 copy-start.56
  1224.8 20.3 %copy-start.1 = (bf16[8,4,1024,16]{2,3,1,0:T(8,128)(2,1)S(1)}, bf16[8,4,1024,16]{2,3,1,0:T(8,128)(2,1)}, u32[]{:S(2)}) copy-start(bf16[8,4,1024,16]{2,3,1,0:T(8,128)(2,1)} %param.30) | copy-start | bytes 3145732
  (15 other events, 30.9 us)
Sparse Core Ops, SparseCore 0:
  10.7 47.1 all-gather.9
  66.8 39.6 all-gather.17
  108.7 32.5 all-gather.15
  143.3 49.0 all-gather.13
  195.3 153.5 all-reduce.9
  350.9 49.2 all-gather.11
  430.8 153.4 all-reduce.13
  624.7 54.5 reduce-scatter.4
  692.7 54.4 reduce-scatter.2
  750.0 31.5 all-reduce.11
  784.6 159.2 all-reduce.15
  948.5 169.8 all-reduce.17
  1120.0 104.8 all-gather.19
